TPU v7x, 32 devices: a whole 2x2x4 slice. The times are simulated.
32 devices in a mesh: meet: 2 (over x), tm: 16 (over z, y, core).
Axes of the slice: x: 2, y: 2, z: 4, core: 2. Of those that a mesh axis runs over, the one named last changes fastest.
Arguments:
- waveform: bfloat16 [8, 327680], P(None, ('meet', 'tm')), parts along dimension 1, may hold values from -16 to 16
- masks: int32 [2, 2048, 257], P(None, ('meet', 'tm')), parts along dimension 1, may hold values from 0 to 255, as said below
- valid: int32 [2], P('meet'), parts along dimension 0, may hold values from 512 to 1024, as said below
- ref_mic: int32 [2], P('meet'), parts along dimension 0, may hold values from 0 to 7
- conv1_w: bfloat16 [9, 256], replicated, may hold values from -2 to 2
- conv1_b: float32 [256], replicated, may hold values from -4 to 4
- conv2_w: bfloat16 [9, 256, 256], replicated, may hold values from -0.125 to 0.125
- conv2_b: float32 [256], replicated, may hold values from -4 to 4
- proj_w: bfloat16 [4864, 256], replicated, may hold values from -0.078125 to 0.078125
- proj_b: float32 [256], replicated, may hold values from -4 to 4
Outputs:
- features: bfloat16 [1, 512, 256], P(None, ('meet', 'tm')), parts along dimension 1
There are 2 independent parts, one for each index of `meet`. A program takes and returns all parts, laid end to end along the dimension named above; an argument that names none is the same for every part. Nothing has to cross between parts.
Inputs may be any that keep to these rules, and one draw needn't show every extreme that they name: `masks`: mask levels; level / 255 is the weight of a time-frequency cell for a speaker or, in the last row, for the noise. `valid`: frames of the meeting that hold speech data; all 1024 in some meetings.
All inputs are finite; a program needn't handle non-finite values.
Results may differ from a plain program's by a relative error of at most 0.003.
The roundings to bfloat16 on the way count: a program that leaves them out, or rounds other values in their place, can miss the bound.
Values may be sent and summed in bfloat16 or wider, within the bound.
A program may use at most 64 MiB of HBM per device.

v0:
```python
import functools
import math

import jax
import jax.numpy as jnp
import numpy as np
from jax import lax
from jax.experimental import pallas as pl
from jax.experimental.pallas import tpu as pltpu
from jax.sharding import PartitionSpec as P

NFFT = 512
HOP = 160
MELS = 80
BINS = NFFT // 2 + 1
LANES = 128
MAIN = BINS - 1
PADDED = MAIN + LANES
SPECTRUM = 2 * MAIN + LANES
GROUP = 4
SPAN = GROUP * HOP
WINDOW = 1024

loading = 0.03
epsilon = 1e-06
sample_rate = 16000.0


def dft_table():
    sample_pos = np.arange(NFFT)
    phase = (sample_pos[:, None] * np.arange(BINS)[None, :] % NFFT).astype(np.float32)
    phase = phase * np.float32(2.0 * math.pi / NFFT)
    ramp = sample_pos.astype(np.float32) * np.float32(2.0 * math.pi / NFFT)
    window = np.float32(0.5) - np.float32(0.5) * np.cos(ramp)
    cosines = window[:, None] * np.cos(phase)
    sines = -window[:, None] * np.sin(phase)
    table = np.zeros((NFFT, SPECTRUM), np.float32)
    table[:, :MAIN] = cosines[:, :MAIN]
    table[:, MAIN : 2 * MAIN] = sines[:, :MAIN]
    table[:, 2 * MAIN :] = cosines[:, MAIN:]
    return table.astype(jnp.bfloat16)


def mel_bank():
    mel_top = 2595.0 * math.log10(1.0 + sample_rate / 2.0 / 700.0)
    points = np.arange(MELS + 2) * (mel_top / (MELS + 1))
    edges_hz = 700.0 * (np.power(10.0, points / 2595.0) - 1.0)
    freq_hz = np.arange(BINS) * (sample_rate / 2.0 / (BINS - 1))
    lower, centre, upper = edges_hz[:-2], edges_hz[1:-1], edges_hz[2:]
    rising = (freq_hz[:, None] - lower[None, :]) / (centre - lower)[None, :]
    falling = (upper[None, :] - freq_hz[:, None]) / (upper - centre)[None, :]
    bank = np.zeros((PADDED, LANES), np.float32)
    bank[:BINS, :MELS] = np.maximum(np.minimum(rising, falling), 0.0)
    return bank


def repeat_table():
    table = np.zeros((LANES, MELS * 8), np.float32)
    for mel in range(MELS):
        table[mel, mel * 8 : mel * 8 + 8] = 1.0
    return table.astype(jnp.bfloat16)


def kernel(
    n,
    valid_ref,
    mic_ref,
    wave_hbm,
    masks_hbm,
    table_hbm,
    bank_hbm,
    repeat_hbm,
    conv1_w_hbm,
    conv1_b_hbm,
    conv2_hbm,
    conv2_b_hbm,
    proj_hbm,
    proj_b_hbm,
    out_ref,
    conv1_w,
    conv1_b,
    conv2_b,
    proj_b,
    wave,
    masks,
    table,
    ext,
    weight,
    spec,
    left,
    right,
    cov,
    part,
    landed,
    packed,
    gathered,
    full,
    bank,
    repeat,
    conv2_w,
    proj_w,
    beam,
    power,
    spread,
    lined,
    kernel_one,
    patches,
    first,
    nearby_send,
    nearby_recv,
    send_one,
    recv_one,
    send_two,
    recv_two,
    loads,
):
    rows, frames = masks.shape[0], masks.shape[1]
    mics, own = wave.shape
    groups = frames // GROUP + 1
    reach = right.shape[1]
    me = lax.axis_index("tm")
    load_wave = pltpu.make_async_copy(wave_hbm, wave, loads.at[0])
    load_table = pltpu.make_async_copy(table_hbm, table, loads.at[1])
    load_masks = pltpu.make_async_copy(masks_hbm, masks, loads.at[2])
    load_wave.start()
    load_table.start()
    load_masks.start()
    load_conv2 = pltpu.make_async_copy(conv2_hbm, conv2_w, loads.at[3])
    load_proj = pltpu.make_async_copy(proj_hbm, proj_w, loads.at[4])
    load_bank = pltpu.make_async_copy(bank_hbm, bank, loads.at[5])
    load_repeat = pltpu.make_async_copy(repeat_hbm, repeat, loads.at[6])
    barrier = pltpu.get_barrier_semaphore()
    for j in range(1, n):
        pl.semaphore_signal(
            barrier,
            inc=1,
            device_id={"tm": lax.rem(me + j, n)},
            device_id_type=pl.DeviceIdType.MESH,
        )

    def transform(chosen):
        spans = jnp.concatenate(
            [ext[:, g * SPAN : g * SPAN + WINDOW] for g in chosen], axis=0
        )
        framed = jnp.concatenate(
            [
                (spans if r == 0 else pltpu.roll(spans, WINDOW - r * HOP, axis=1))[:, :NFFT]
                for r in range(GROUP)
            ],
            axis=0,
        ).astype(jnp.bfloat16)
        return jnp.dot(framed, table[...], preferred_element_type=jnp.float32)

    load_wave.wait()
    ext[:, SPAN : SPAN + own] = wave[...].astype(jnp.float32)
    load_table.wait()
    inner = list(range(1, groups - 1))
    found = transform(inner)
    width = len(inner) * mics
    for r in range(GROUP):
        spec[(r * groups + 1) * mics : (r * groups + 1) * mics + width, :] = found[
            r * width : (r + 1) * width
        ]

    pl.semaphore_wait(barrier, n - 1)
    to_right = pltpu.make_async_remote_copy(
        src_ref=wave_hbm.at[:, own - SPAN :],
        dst_ref=left,
        send_sem=nearby_send.at[0],
        recv_sem=nearby_recv.at[0],
        device_id={"tm": lax.rem(me + 1, n)},
        device_id_type=pl.DeviceIdType.MESH,
    )
    to_left = pltpu.make_async_remote_copy(
        src_ref=wave_hbm.at[:, :reach],
        dst_ref=right,
        send_sem=nearby_send.at[1],
        recv_sem=nearby_recv.at[1],
        device_id={"tm": lax.rem(me + n - 1, n)},
        device_id_type=pl.DeviceIdType.MESH,
    )
    to_right.start()
    to_left.start()
    small = [
        pltpu.make_async_copy(source, held, loads.at[7 + i])
        for i, (source, held) in enumerate(
            (
                (conv1_w_hbm, conv1_w),
                (conv1_b_hbm, conv1_b),
                (conv2_b_hbm, conv2_b),
                (proj_b_hbm, proj_b),
            )
        )
    ]
    for load in small:
        load.start()
    load_bank.start()
    load_repeat.start()
    load_conv2.start()
    load_proj.start()

    load_masks.wait()
    limit = valid_ref[0] - me * frames
    alive = lax.broadcasted_iota(jnp.int32, (frames, MAIN), 0) < limit
    for k in range(rows):
        level = masks[k].astype(jnp.float32) * (1.0 / 255.0)
        weight[k, :, :MAIN] = jnp.where(alive, level[:, :MAIN], 0.0)
        weight[k, :, MAIN:] = jnp.where(
            alive[:, :LANES], jnp.broadcast_to(level[:, MAIN:], (frames, LANES)), 0.0
        )

    half = mics // 2
    low = lax.broadcasted_iota(jnp.int32, (mics, LANES), 0) < half

    def frames_of(h):
        first_row = h * 2 * GROUP
        if not isinstance(h, int):
            first_row = pl.multiple_of(first_row, 2 * GROUP)
        places = []
        for i in range(2 * GROUP):
            at = ((i % GROUP) * groups + 1 + 2 * h + i // GROUP) * mics
            if not isinstance(h, int):
                at = pl.multiple_of(at, mics)
            places.append(pl.ds(at, mics))
        return pl.ds(first_row, 2 * GROUP), places

    def add_block(h, totals, block):
        totals = list(totals)
        lanes = pl.ds(block * LANES, LANES)
        lanes_im = pl.ds(MAIN + block * LANES, LANES)
        span, places = frames_of(h)
        held = [weight[k, span, lanes] for k in range(rows)]
        for i, at in enumerate(places):
            re = spec[at, lanes]
            im = spec[at, lanes_im]
            w = [held[k][i : i + 1] for k in range(rows)]
            place = 0
            for d in range(half + 1):
                if d == 0:
                    products = [re * re + im * im]
                else:
                    re_n = pltpu.roll(re, mics - d, axis=0)
                    im_n = pltpu.roll(im, mics - d, axis=0)
                    real = re * re_n + im * im_n
                    imag = im * re_n - re * im_n
                    products = [real, imag] if d < half else [jnp.where(low, real, imag)]
                for product in products:
                    for k in range(rows):
                        slot = k * mics + place
                        totals[slot] = totals[slot] + w[k] * product
                    place += 1
        return tuple(totals)

    def add_last_bin(h, totals):
        totals = list(totals)
        span, places = frames_of(h)
        held = [weight[k, span, pl.ds(MAIN, LANES)] for k in range(rows)]
        for i, at in enumerate(places):
            re = spec[at, pl.ds(2 * MAIN, LANES)]
            for d in range(half + 1):
                product = re * (re if d == 0 else pltpu.roll(re, mics - d, axis=0))
                for k in range(rows):
                    slot = k * (half + 1) + d
                    totals[slot] = totals[slot] + held[k][i : i + 1] * product
        return tuple(totals)

    blocks = frames // (2 * GROUP)
    tiles = MAIN // LANES
    planes = rows * mics
    extra = rows * (half + 1)
    adders = [functools.partial(add_block, block=block) for block in range(tiles)]
    adders.append(add_last_bin)
    counts = [planes] * tiles + [extra]
    for block in range(tiles + 1):
        zeros = tuple(jnp.zeros((mics, LANES), jnp.float32) for _ in range(counts[block]))
        totals = lax.fori_loop(0, blocks - 1, adders[block], zeros)
        for slot in range(counts[block]):
            cov[block, slot] = totals[slot]

    to_right.wait_recv()
    to_left.wait_recv()
    ext[:, :SPAN] = jnp.where(me > 0, left[...].astype(jnp.float32), 0.0)
    ext[:, SPAN + own :] = jnp.where(me < n - 1, right[...].astype(jnp.float32), 0.0)
    found = transform([0, groups - 1])
    for r in range(GROUP):
        for i, g in enumerate((0, groups - 1)):
            at = (r * 2 + i) * mics
            spec[(r * groups + g) * mics : (r * groups + g + 1) * mics, :] = found[at : at + mics]

    lane = lax.broadcasted_iota(jnp.int32, (mics, LANES), 1)
    sub = lax.broadcasted_iota(jnp.int32, (mics, LANES), 0)
    width = MAIN // n
    per_tile = LANES // width
    deep = -(-planes // per_tile)

    def turned(value, amount):
        amount = amount % LANES
        return pltpu.roll(value, amount, axis=1) if amount else value

    totals = add_last_bin(blocks - 1, tuple(cov[tiles, slot] for slot in range(extra)))
    line = jnp.zeros((mics, LANES), jnp.float32)
    for slot in range(extra):
        line = jnp.where(lane == mics * slot + sub, totals[slot], line)
    line = jnp.sum(line, axis=0, keepdims=True)
    for to in range(n):
        part[to, deep * mics : deep * mics + 1, :] = line
    for block in range(tiles):
        totals = adders[block](blocks - 1, tuple(cov[block, slot] for slot in range(planes)))
        for slot in range(planes):
            cov[block, slot] = totals[slot]
        for to in range(block * per_tile, (block + 1) * per_tile):
            for tile in range(deep):
                packing = jnp.zeros((mics, LANES), jnp.float32)
                for i in range(min(per_tile, planes - tile * per_tile)):
                    moved = turned(cov[block, tile * per_tile + i], (i - to % per_tile) * width)
                    packing = moved if i == 0 else jnp.where(lane // width == i, moved, packing)
                part[to, tile * mics : (tile + 1) * mics, :] = packing

    sent_one = []
    for j in range(1, n):
        to = lax.rem(me + j, n)
        copy = pltpu.make_async_remote_copy(
            src_ref=part.at[to],
            dst_ref=landed.at[j],
            send_sem=send_one.at[j],
            recv_sem=recv_one.at[j],
            device_id={"tm": to},
            device_id_type=pl.DeviceIdType.MESH,
        )
        copy.start()
        sent_one.append(copy)

    for load in small:
        load.wait()
    channels = conv1_w.shape[1]
    kernel_one[...] = jnp.zeros_like(kernel_one)
    for a in range(3):
        for b in range(3):
            tap = conv1_w[3 * a + b : 3 * a + b + 1, :].astype(jnp.float32)
            for late in range(3):
                at = b * 8 + 2 * late + a
                kernel_one[at : at + 1, late * channels : (late + 1) * channels] = tap
    power[...] = jnp.zeros_like(power)
    lined[...] = jnp.zeros_like(lined)

    total = part[me]
    for j in range(1, n):
        sent_one[j - 1].wait_recv()
        total = total + landed[j]
    line = total[deep * mics : deep * mics + 1]
    lasts = [
        jnp.sum(jnp.where(lane == mics * slot + sub, line, 0.0), axis=1, keepdims=True)
        for slot in range(extra)
    ]
    whole = []
    for slot in range(planes):
        tile = slot // per_tile
        plane = turned(total[tile * mics : (tile + 1) * mics], -(slot % per_tile) * width)
        k, place = slot // mics, slot % mics
        d = (place + 1) // 2
        if place == 0 or (place % 2 == 1 and d < half):
            at_last = lasts[k * (half + 1) + d]
        elif d == half:
            at_last = jnp.where(low, lasts[k * (half + 1) + d], 0.0)
        else:
            at_last = jnp.zeros((mics, LANES), jnp.float32)
        whole.append(jnp.where(lane == width, at_last, plane))
    solved = solve(whole, mics, full, mic_ref[0])
    for i in range(2):
        value = jnp.where(lane < width, solved[i], 0.0)
        for step in (1, 2, 4):
            value = value + turned(value, step * width)
        value = jnp.where(lane // width == sub, value, 0.0)
        packed[i : i + 1, :] = jnp.sum(value, axis=0, keepdims=True)
    sent_two = []
    for j in range(1, n):
        copy = pltpu.make_async_remote_copy(
            src_ref=packed,
            dst_ref=gathered.at[me],
            send_sem=send_two.at[j],
            recv_sem=recv_two.at[j],
            device_id={"tm": lax.rem(me + j, n)},
            device_id_type=pl.DeviceIdType.MESH,
        )
        copy.start()
        sent_two.append(copy)
    gathered[me] = packed[...]
    for i in range(2):
        at_last = jnp.sum(jnp.where(lane == width, solved[i], 0.0), axis=1, keepdims=True)
        beam[i, :, MAIN:] = jnp.broadcast_to(at_last, (mics, LANES))
    to_right.wait_send()
    to_left.wait_send()
    for j in range(1, n):
        sent_two[j - 1].wait_recv()
    for i in range(2):
        for block in range(tiles):
            joined = jnp.zeros((mics, LANES), jnp.float32)
            for t in range(per_tile):
                row = gathered[block * per_tile + t, i : i + 1, :]
                value = jnp.where(lane // width == sub, row, 0.0)
                for step in (1, 2, 4):
                    value = value + turned(value, step * width)
                if mics * width < LANES:
                    value = turned(value, (t - mics + 1) * width)
                joined = jnp.where(lane // width == t, value, joined)
            beam[i, :, block * LANES : (block + 1) * LANES] = joined

    load_bank.wait()
    load_repeat.wait()
    stem(
        valid_ref[0],
        spec,
        bank,
        repeat,
        conv1_b,
        load_conv2,
        conv2_w,
        conv2_b,
        load_proj,
        proj_w,
        proj_b,
        out_ref,
        beam,
        power,
        spread,
        lined,
        kernel_one,
        patches,
        first,
    )
    for j in range(1, n):
        sent_one[j - 1].wait_send()
        sent_two[j - 1].wait_send()


def solve(planes, mics, full, ref):
    half = mics // 2
    for k in range(2):
        for m in range(mics):
            for d in range(half + 1):
                n = (m + d) % mics
                if d == half and m >= half:
                    continue

                def row(plane, at):
                    return planes[k * mics + plane][at : at + 1]

                if d == 0:
                    full[2 * k, m, m : m + 1, :] = row(0, m)
                    full[2 * k + 1, m, m : m + 1, :] = jnp.zeros((1, LANES), jnp.float32)
                    continue
                if d < half:
                    real, imag = row(2 * d - 1, m), row(2 * d, m)
                else:
                    real, imag = row(2 * d - 1, m), -row(2 * d - 1, m + half)
                full[2 * k, m, n : n + 1, :] = real
                full[2 * k + 1, m, n : n + 1, :] = imag
                full[2 * k, n, m : m + 1, :] = real
                full[2 * k + 1, n, m : m + 1, :] = -imag
    answer_re = [full[0, m] for m in range(mics)]
    answer_im = [full[1, m] for m in range(mics)]
    matrix_re = [full[2, m] for m in range(mics)]
    matrix_im = [full[3, m] for m in range(mics)]
    index = lax.broadcasted_iota(jnp.int32, (mics, LANES), 0)
    spread = matrix_re[0][0:1]
    for m in range(1, mics):
        spread = spread + matrix_re[m][m : m + 1]
    ridge = loading * spread / mics + epsilon
    matrix_re = [
        jnp.where(index == m, matrix_re[m] + ridge, matrix_re[m]) for m in range(mics)
    ]
    for p in range(mics):
        pivot_re, pivot_im = matrix_re[p][p : p + 1], matrix_im[p][p : p + 1]
        scale = 1.0 / (pivot_re * pivot_re + pivot_im * pivot_im)
        inverse_re, inverse_im = pivot_re * scale, -pivot_im * scale
        lead_re = matrix_re[p] * inverse_re - matrix_im[p] * inverse_im
        lead_im = matrix_re[p] * inverse_im + matrix_im[p] * inverse_re
        head_re = answer_re[p] * inverse_re - answer_im[p] * inverse_im
        head_im = answer_re[p] * inverse_im + answer_im[p] * inverse_re
        for m in range(mics):
            if m == p:
                continue
            column_re, column_im = matrix_re[m][p : p + 1], matrix_im[m][p : p + 1]
            matrix_re[m] = matrix_re[m] - (column_re * lead_re - column_im * lead_im)
            matrix_im[m] = matrix_im[m] - (column_re * lead_im + column_im * lead_re)
            answer_re[m] = answer_re[m] - (column_re * head_re - column_im * head_im)
            answer_im[m] = answer_im[m] - (column_re * head_im + column_im * head_re)
        matrix_re[p], matrix_im[p] = lead_re, lead_im
        answer_re[p], answer_im[p] = head_re, head_im
    trace = answer_re[0][0:1]
    for m in range(1, mics):
        trace = trace + answer_re[m][m : m + 1]
    scale = 1.0 / (trace + epsilon)
    picked = index == ref
    beam_re = jnp.zeros((mics, LANES), jnp.float32)
    beam_im = jnp.zeros((mics, LANES), jnp.float32)
    for m in range(mics):
        real = jnp.sum(jnp.where(picked, answer_re[m], 0.0), axis=0, keepdims=True)
        imag = jnp.sum(jnp.where(picked, answer_im[m], 0.0), axis=0, keepdims=True)
        beam_re = jnp.where(index == m, real * scale, beam_re)
        beam_im = jnp.where(index == m, imag * scale, beam_im)
    return beam_re, beam_im


def row_sums(values):
    count = len(values)
    sub = lax.broadcasted_iota(jnp.int32, values[0].shape, 0)
    step = count // 2
    while step:
        upper = sub // step % 2 == 1
        values = [
            jnp.where(
                upper,
                values[i + step] + pltpu.roll(values[i + step], step, axis=0),
                values[i] + pltpu.roll(values[i], count - step, axis=0),
            )
            for i in range(step)
        ]
        step //= 2
    return values[0]


def stem(
    valid,
    spec,
    bank,
    repeat,
    conv1_b,
    load_conv2,
    conv2_w,
    conv2_b,
    load_proj,
    proj_w,
    proj_b,
    out_ref,
    beam,
    power,
    spread,
    lined,
    kernel_one,
    patches,
    first,
):
    mics = beam.shape[1]
    quarter = out_ref.shape[0]
    groups = quarter + 1
    frames = quarter * GROUP
    stride = power.shape[0] // GROUP
    channels = conv2_w.shape[1]
    q_first = (MELS - 3) // 2 + 1
    q_second = (q_first - 3) // 2 + 1
    position = lax.axis_index("tm")
    for block in range(PADDED // LANES):
        lanes = pl.ds(block * LANES, LANES)
        beam_re = beam[0, :, lanes]
        beam_im = beam[1, :, lanes]

        def products(r, g):
            at = slice((r * groups + g) * mics, (r * groups + g + 1) * mics)
            if block < MAIN // LANES:
                re = spec[at, lanes]
                im = spec[at, pl.ds(MAIN + block * LANES, LANES)]
                return beam_re * re + beam_im * im, beam_re * im - beam_im * re
            re = spec[at, pl.ds(2 * MAIN, LANES)]
            return beam_re * re, -beam_im * re

        for r in range(GROUP):
            for g in range(0, groups - mics + 1, mics):
                pairs = [products(r, g + i) for i in range(mics)]
                real = row_sums([pair[0] for pair in pairs])
                imag = row_sums([pair[1] for pair in pairs])
                at = r * stride + g
                power[at : at + mics, lanes] = real * real + imag * imag
            for g in range(groups - groups % mics, groups):
                real, imag = products(r, g)
                real = jnp.sum(real, axis=0, keepdims=True)
                imag = jnp.sum(imag, axis=0, keepdims=True)
                at = r * stride + g
                power[at : at + 1, lanes] = real * real + imag * imag

    melspec = (
        jnp.dot(
            power[:, :MAIN],
            bank[:MAIN, :],
            preferred_element_type=jnp.float32,
            precision=lax.Precision.HIGHEST,
        )
        + power[:, MAIN:] * bank[MAIN : MAIN + 1, :]
    )
    row = lax.broadcasted_iota(jnp.int32, melspec.shape, 0)
    frame = position * frames + (row % stride - 1) * GROUP + row // stride
    alive = (frame >= 0) & (frame < valid)
    logmel = jnp.where(alive, jnp.log(melspec + epsilon), 0.0).astype(jnp.bfloat16)
    spread[...] = jnp.dot(logmel, repeat[...], preferred_element_type=jnp.float32)
    width = spread.shape[1]
    phase = lax.broadcasted_iota(jnp.int32, (quarter, width), 1) % 8
    mixed = jnp.zeros((quarter, width), jnp.float32)
    for u in range(7):
        start = (u + 1) % GROUP * stride + (u + 1) // GROUP
        mixed = jnp.where(phase == u, spread[start : start + quarter, :], mixed)
    lined[:, :width] = mixed
    order = list(range(0, q_first, 2)) + list(range(1, q_first, 2))
    for place, q in enumerate(order):
        base = 16 * q // LANES * LANES
        shift = 16 * q - base
        two = lined[:, base : base + 2 * LANES]
        if shift:
            two = pltpu.roll(two, 2 * LANES - shift, axis=1)
        patches[place * quarter : (place + 1) * quarter, :] = two[:, :LANES].astype(jnp.bfloat16)

    kernel_bf = kernel_one[...].astype(jnp.bfloat16)
    for late in range(3):
        lanes = slice(late * channels, (late + 1) * channels)
        one = jnp.dot(patches[...], kernel_bf[:, lanes], preferred_element_type=jnp.float32)
        one = jnp.maximum(one + conv1_b[...], 0.0)
        if late == 0:
            step = lax.broadcasted_iota(jnp.int32, one.shape, 0) % quarter
            one = jnp.where((step == 0) & (position == 0), 0.0, one)
        first[:, lanes] = one.astype(jnp.bfloat16)

    load_conv2.wait()
    evens = (q_first + 1) // 2
    summed = jnp.zeros((q_second * quarter, channels), jnp.float32)
    for b in range(3):
        start = {0: 0, 1: evens, 2: 1}[b] * quarter
        for late in range(3):
            summed = summed + jnp.dot(
                first[start : start + q_second * quarter, late * channels : (late + 1) * channels],
                conv2_w[3 * late + b],
                preferred_element_type=jnp.float32,
            )
    second = jnp.maximum(summed + conv2_b[...], 0.0).astype(jnp.bfloat16)
    load_proj.wait()
    out = jnp.zeros((quarter, out_ref.shape[1]), jnp.float32)
    for r in range(q_second):
        out = out + jnp.dot(
            second[r * quarter : (r + 1) * quarter],
            proj_w[r * channels : (r + 1) * channels, :],
            preferred_element_type=jnp.float32,
        )
    out_row = lax.broadcasted_iota(jnp.int32, out.shape, 0) + position * quarter
    out = jnp.where(GROUP * out_row < valid, out + proj_b[...], 0.0)
    out_ref[...] = out


def per_device(
    n, waveform, masks, valid, ref_mic, conv1_w, conv1_b, conv2_w, conv2_b, proj_w, proj_b
):
    mics, own = waveform.shape
    rows, frames = masks.shape[0], masks.shape[1]
    groups = frames // GROUP + 1
    quarter = frames // GROUP
    channels = conv1_w.shape[1]
    model = proj_w.shape[1]
    reach = WINDOW - SPAN
    vmem = pl.BlockSpec(memory_space=pltpu.VMEM)
    smem = pl.BlockSpec(memory_space=pltpu.SMEM)
    anywhere = pl.BlockSpec(memory_space=pl.ANY)
    planes = rows * mics
    deep = -(-planes * (MAIN // n) // LANES)
    tall = deep * mics + 1
    stride = -(-groups // 8) * 8
    q_first = (MELS - 3) // 2 + 1
    q_count = q_first * quarter
    features = pl.pallas_call(
        functools.partial(kernel, n),
        out_shape=jax.ShapeDtypeStruct((quarter, model), jnp.float32),
        in_specs=[smem] * 2 + [anywhere] * 5 + [anywhere, anywhere, anywhere, anywhere, anywhere, anywhere],
        out_specs=vmem,
        scratch_shapes=[
            pltpu.VMEM(conv1_w.shape, conv1_w.dtype),
            pltpu.VMEM((1, channels), jnp.float32),
            pltpu.VMEM((1, channels), jnp.float32),
            pltpu.VMEM((1, model), jnp.float32),
            pltpu.VMEM(waveform.shape, waveform.dtype),
            pltpu.VMEM(masks.shape, masks.dtype),
            pltpu.VMEM((NFFT, SPECTRUM), jnp.bfloat16),
            pltpu.VMEM((mics, SPAN + own + reach), jnp.float32),
            pltpu.VMEM((rows, frames, PADDED), jnp.float32),
            pltpu.VMEM((GROUP * groups * mics, SPECTRUM), jnp.float32),
            pltpu.VMEM((mics, SPAN), waveform.dtype),
            pltpu.VMEM((mics, reach), waveform.dtype),
            pltpu.VMEM((PADDED // LANES, planes, mics, LANES), jnp.float32),
            pltpu.VMEM((n, tall, LANES), jnp.float32),
            pltpu.VMEM((n, tall, LANES), jnp.float32),
            pltpu.VMEM((2, LANES), jnp.float32),
            pltpu.VMEM((n, 2, LANES), jnp.float32),
            pltpu.VMEM((4, mics, mics, LANES), jnp.float32),
            pltpu.VMEM((PADDED, LANES), jnp.float32),
            pltpu.VMEM((LANES, MELS * 8), jnp.bfloat16),
            pltpu.VMEM(conv2_w.shape, jnp.bfloat16),
            pltpu.VMEM(proj_w.shape, jnp.bfloat16),
            pltpu.VMEM((2, mics, PADDED), jnp.float32),
            pltpu.VMEM((GROUP * stride, PADDED), jnp.float32),
            pltpu.VMEM((GROUP * stride, MELS * 8), jnp.float32),
            pltpu.VMEM((quarter, MELS * 8 + LANES), jnp.float32),
            pltpu.VMEM((LANES, 3 * channels), jnp.float32),
            pltpu.VMEM((q_count, LANES), jnp.bfloat16),
            pltpu.VMEM((q_count, 3 * channels), jnp.bfloat16),
            pltpu.SemaphoreType.DMA((2,)),
            pltpu.SemaphoreType.DMA((2,)),
            pltpu.SemaphoreType.DMA((n,)),
            pltpu.SemaphoreType.DMA((n,)),
            pltpu.SemaphoreType.DMA((n,)),
            pltpu.SemaphoreType.DMA((n,)),
            pltpu.SemaphoreType.DMA((11,)),
        ],
        compiler_params=pltpu.CompilerParams(
            collective_id=0, has_side_effects=True
        ),
    )(
        valid,
        ref_mic,
        waveform,
        masks,
        jnp.asarray(dft_table()),
        jnp.asarray(mel_bank()),
        jnp.asarray(repeat_table()),
        conv1_w,
        conv1_b[None],
        conv2_w,
        conv2_b[None],
        proj_w,
        proj_b[None],
    )
    return features.astype(jnp.bfloat16)[None]


def solution(mesh):
    return jax.shard_map(
        functools.partial(per_device, mesh.shape["tm"]),
        mesh=mesh,
        in_specs=(
            P(None, ("meet", "tm")),
            P(None, ("meet", "tm"), None),
            P("meet"),
            P("meet"),
            P(),
            P(),
            P(),
            P(),
            P(),
            P(),
        ),
        out_specs=P(None, ("meet", "tm"), None),
        check_vma=False,
    )
```

profile of v0, /device:TPU:0, one launch (start us, length us, event | category | flops | bytes accessed | tf_op | source)
XLA Modules:
  0.0 26.2 jit_solution(4555667485094827767)
XLA Ops:
  1.3 23.6 %shard_map.127 = f32[16,256]{1,0:T(8,128)} custom-call(s32[1]{0:T(128)S(6)} %copy.14.valid_ref, s32[1]{0:T(128)S(6)} %copy.15.mic_ref, bf16[8,10240]{1,0:T(8,128)(2,1)} %wave_hbm.1, s32[2,64,257]{2,1,0:T(8,128)} %masks_hbm.1, bf16[512,640]{1,0:T(8,128)(2,1)} %constant.6.clone.table_hbm, f32[384,128]{1,0:T(8,128)} %constant.7.clone.bank_hbm, ...), custom_call_target="tpu_custom_call" | custom-call | tf_op jit(solution)/shard_map/pallas_call | solution.py:665
  24.9 1.3 %convert_bitcast_fusion = bf16[1,16,256]{2,1,0:T(8,128)(2,1)} fusion(f32[16,256]{1,0:T(8,128)} %shard_map.127), kind=kLoop, calls=%fused_computation | loop fusion | flops 4096 | bytes 24576 | tf_op jit(solution)/shard_map/broadcast_in_dim | solution.py:726
where the time goes:
time: 26.4 us; the launch traced here: 26.2 us
  Pallas kernels  23.6 us (89%)
  other arithmetic  1.32 us (5%)
  between operations  1.3 us (5%)
    pallas_call x1, Pallas kernels, per_device(): pl.pallas_call(functools.partial(kernel, n), out_shape=jax.ShapeDtypeStru...  23.6 us
    broadcast_in_dim x1, other arithmetic, per_device(): return features.astype(jnp.bfloat16)[None]  1.32 us

commit v1 on v0

--- a/solution.py
+++ b/solution.py
@@ -655,7 +655,7 @@
     reach = WINDOW - SPAN
     vmem = pl.BlockSpec(memory_space=pltpu.VMEM)
     smem = pl.BlockSpec(memory_space=pltpu.SMEM)
-    anywhere = pl.BlockSpec(memory_space=pl.ANY)
+    anywhere = pl.BlockSpec(memory_space=pltpu.HBM)
     planes = rows * mics
     deep = -(-planes * (MAIN // n) // LANES)
     tall = deep * mics + 1
@@ -706,22 +706,27 @@
             pltpu.SemaphoreType.DMA((11,)),
         ],
         compiler_params=pltpu.CompilerParams(
-            collective_id=0, has_side_effects=True
+            collective_id=0, has_side_effects=True, vmem_limit_bytes=16 << 20
         ),
     )(
         valid,
         ref_mic,
-        waveform,
-        masks,
-        jnp.asarray(dft_table()),
-        jnp.asarray(mel_bank()),
-        jnp.asarray(repeat_table()),
-        conv1_w,
-        conv1_b[None],
-        conv2_w,
-        conv2_b[None],
-        proj_w,
-        proj_b[None],
+        *(
+            pltpu.with_memory_space_constraint(held, pltpu.HBM)
+            for held in (
+                waveform,
+                masks,
+                jnp.asarray(dft_table()),
+                jnp.asarray(mel_bank()),
+                jnp.asarray(repeat_table()),
+                conv1_w,
+                conv1_b[None],
+                conv2_w,
+                conv2_b[None],
+                proj_w,
+                proj_b[None],
+            )
+        ),
     )
     return features.astype(jnp.bfloat16)[None]
 

time: 26.4 us -> 25 us (0.947)
  other arithmetic: 1.32 us -> 0.6 us
  Pallas kernels: 23.6 us -> 23 us
    broadcast_in_dim x1, other arithmetic: 1.32 us -> 0.6 us  [per_device(): return features.astype(jnp.bfloat16)[None]]
    pallas_call x1, Pallas kernels: 23.6 us -> 23 us  [per_device(): pl.pallas_call(functools.partial(kernel, n), out_shape=jax.ShapeDtypeStru...]
where the time goes in v1:
time: 25 us; the launch traced here: 24.9 us
  Pallas kernels  23 us (92%)
  between operations  1.3 us (5%)
  other arithmetic  0.6 us (2%)
    pallas_call x1, Pallas kernels, per_device(): pl.pallas_call(functools.partial(kernel, n), out_shape=jax.ShapeDtypeStru...  23 us
    broadcast_in_dim x1, other arithmetic, per_device(): return features.astype(jnp.bfloat16)[None]  0.6 us

profile of v1, /device:TPU:0, one launch (start us, length us, event | category | flops | bytes accessed | tf_op | source)
XLA Modules:
  0.0 24.9 jit_solution(8600071200707531167)
XLA Ops:
  1.3 23.0 %shard_map.127 = f32[16,256]{1,0:T(8,128)S(1)} custom-call(s32[1]{0:T(128)S(6)} %copy.14.valid_ref, s32[1]{0:T(128)S(6)} %copy.15.mic_ref, bf16[8,10240]{1,0:T(8,128)(2,1)} %wave_hbm.1, s32[2,64,257]{2,1,0:T(8,128)} %masks_hbm.1, bf16[512,640]{1,0:T(8,128)(2,1)} %constant.6.clone.table_hbm, f32[384,128]{1,0:T(8,128)} %constant.7.clone.bank_hbm, ...), custom_call_target="tpu_custom_call" | custom-call | tf_op jit(solution)/shard_map/pallas_call | solution.py:665
  24.3 0.6 %convert_bitcast_fusion = bf16[1,16,256]{2,1,0:T(8,128)(2,1)} fusion(f32[16,256]{1,0:T(8,128)S(1)} %shard_map.127), kind=kLoop, calls=%fused_computation | loop fusion | flops 4096 | bytes 24576 | tf_op jit(solution)/shard_map/broadcast_in_dim | solution.py:731

commit v2 on v1

--- a/solution.py
+++ b/solution.py
@@ -20,6 +20,7 @@
 GROUP = 4
 SPAN = GROUP * HOP
 WINDOW = 1024
+SOLVERS = 8
 
 loading = 0.03
 epsilon = 1e-06
@@ -119,6 +120,9 @@
     groups = frames // GROUP + 1
     reach = right.shape[1]
     me = lax.axis_index("tm")
+    solvers = part.shape[0]
+    base = (n - solvers) // 2
+    solving = (me >= base) & (me < base + solvers)
     load_wave = pltpu.make_async_copy(wave_hbm, wave, loads.at[0])
     load_table = pltpu.make_async_copy(table_hbm, table, loads.at[1])
     load_masks = pltpu.make_async_copy(masks_hbm, masks, loads.at[2])
@@ -130,39 +134,37 @@
     load_bank = pltpu.make_async_copy(bank_hbm, bank, loads.at[5])
     load_repeat = pltpu.make_async_copy(repeat_hbm, repeat, loads.at[6])
     barrier = pltpu.get_barrier_semaphore()
-    for j in range(1, n):
+
+    def greet(to):
         pl.semaphore_signal(
             barrier,
             inc=1,
-            device_id={"tm": lax.rem(me + j, n)},
+            device_id={"tm": to},
             device_id_type=pl.DeviceIdType.MESH,
         )
 
-    def transform(chosen):
-        spans = jnp.concatenate(
-            [ext[:, g * SPAN : g * SPAN + WINDOW] for g in chosen], axis=0
-        )
-        framed = jnp.concatenate(
-            [
-                (spans if r == 0 else pltpu.roll(spans, WINDOW - r * HOP, axis=1))[:, :NFFT]
-                for r in range(GROUP)
-            ],
-            axis=0,
-        ).astype(jnp.bfloat16)
-        return jnp.dot(framed, table[...], preferred_element_type=jnp.float32)
-
-    load_wave.wait()
-    ext[:, SPAN : SPAN + own] = wave[...].astype(jnp.float32)
-    load_table.wait()
-    inner = list(range(1, groups - 1))
-    found = transform(inner)
-    width = len(inner) * mics
-    for r in range(GROUP):
-        spec[(r * groups + 1) * mics : (r * groups + 1) * mics + width, :] = found[
-            r * width : (r + 1) * width
-        ]
-
-    pl.semaphore_wait(barrier, n - 1)
+    @pl.when(solving)
+    def _():
+        for j in range(1, n):
+            greet(lax.rem(me + j, n))
+
+    @pl.when((me > 0) & jnp.logical_not(solving))
+    def _():
+        greet(me - 1)
+
+    @pl.when((me < n - 1) & jnp.logical_not(solving))
+    def _():
+        greet(me + 1)
+
+    def counted(here):
+        return jnp.where(here, 1, 0).astype(jnp.int32)
+
+    greeted = (
+        solvers
+        - counted(solving)
+        + counted((me > 0) & ((me - 1 < base) | (me - 1 >= base + solvers)))
+        + counted((me < n - 1) & ((me + 1 < base) | (me + 1 >= base + solvers)))
+    )
     to_right = pltpu.make_async_remote_copy(
         src_ref=wave_hbm.at[:, own - SPAN :],
         dst_ref=left,
@@ -179,8 +181,52 @@
         device_id={"tm": lax.rem(me + n - 1, n)},
         device_id_type=pl.DeviceIdType.MESH,
     )
-    to_right.start()
-    to_left.start()
+
+    def meet():
+        pl.semaphore_wait(barrier, greeted)
+
+        @pl.when(me > 0)
+        def _():
+            to_left.start()
+
+        @pl.when(me < n - 1)
+        def _():
+            to_right.start()
+
+    late = me >= n // 2
+
+    @pl.when(late)
+    def _():
+        meet()
+
+    def transform(chosen):
+        spans = jnp.concatenate(
+            [ext[:, g * SPAN : g * SPAN + WINDOW] for g in chosen], axis=0
+        )
+        framed = jnp.concatenate(
+            [
+                (spans if r == 0 else pltpu.roll(spans, WINDOW - r * HOP, axis=1))[:, :NFFT]
+                for r in range(GROUP)
+            ],
+            axis=0,
+        ).astype(jnp.bfloat16)
+        return jnp.dot(framed, table[...], preferred_element_type=jnp.float32)
+
+    load_wave.wait()
+    ext[:, SPAN : SPAN + own] = wave[...].astype(jnp.float32)
+    load_table.wait()
+    inner = list(range(1, groups - 1))
+    found = transform(inner)
+    width = len(inner) * mics
+    for r in range(GROUP):
+        spec[(r * groups + 1) * mics : (r * groups + 1) * mics + width, :] = found[
+            r * width : (r + 1) * width
+        ]
+
+    @pl.when(jnp.logical_not(late))
+    def _():
+        meet()
+
     small = [
         pltpu.make_async_copy(source, held, loads.at[7 + i])
         for i, (source, held) in enumerate(
@@ -277,10 +323,24 @@
         for slot in range(counts[block]):
             cov[block, slot] = totals[slot]
 
-    to_right.wait_recv()
-    to_left.wait_recv()
-    ext[:, :SPAN] = jnp.where(me > 0, left[...].astype(jnp.float32), 0.0)
-    ext[:, SPAN + own :] = jnp.where(me < n - 1, right[...].astype(jnp.float32), 0.0)
+    @pl.when(me > 0)
+    def _():
+        to_right.wait_recv()
+        ext[:, :SPAN] = left[...].astype(jnp.float32)
+
+    @pl.when(me == 0)
+    def _():
+        ext[:, :SPAN] = jnp.zeros((mics, SPAN), jnp.float32)
+
+    @pl.when(me < n - 1)
+    def _():
+        to_left.wait_recv()
+        ext[:, SPAN + own :] = right[...].astype(jnp.float32)
+
+    @pl.when(me == n - 1)
+    def _():
+        ext[:, SPAN + own :] = jnp.zeros((mics, reach), jnp.float32)
+
     found = transform([0, groups - 1])
     for r in range(GROUP):
         for i, g in enumerate((0, groups - 1)):
@@ -289,7 +349,7 @@
 
     lane = lax.broadcasted_iota(jnp.int32, (mics, LANES), 1)
     sub = lax.broadcasted_iota(jnp.int32, (mics, LANES), 0)
-    width = MAIN // n
+    width = MAIN // solvers
     per_tile = LANES // width
     deep = -(-planes // per_tile)
 
@@ -302,7 +362,7 @@
     for slot in range(extra):
         line = jnp.where(lane == mics * slot + sub, totals[slot], line)
     line = jnp.sum(line, axis=0, keepdims=True)
-    for to in range(n):
+    for to in range(solvers):
         part[to, deep * mics : deep * mics + 1, :] = line
     for block in range(tiles):
         totals = adders[block](blocks - 1, tuple(cov[block, slot] for slot in range(planes)))
@@ -316,19 +376,21 @@
                     packing = moved if i == 0 else jnp.where(lane // width == i, moved, packing)
                 part[to, tile * mics : (tile + 1) * mics, :] = packing
 
-    sent_one = []
-    for j in range(1, n):
-        to = lax.rem(me + j, n)
-        copy = pltpu.make_async_remote_copy(
+    def parcel(to, offset):
+        return pltpu.make_async_remote_copy(
             src_ref=part.at[to],
-            dst_ref=landed.at[j],
-            send_sem=send_one.at[j],
-            recv_sem=recv_one.at[j],
-            device_id={"tm": to},
+            dst_ref=landed.at[offset],
+            send_sem=send_one.at[to],
+            recv_sem=recv_one.at[offset],
+            device_id={"tm": base + to},
             device_id_type=pl.DeviceIdType.MESH,
         )
-        copy.start()
-        sent_one.append(copy)
+
+    for to in range(solvers):
+
+        @pl.when(me != base + to)
+        def _():
+            parcel(to, lax.rem(base + to + n - me, n)).start()
 
     for load in small:
         load.wait()
@@ -343,67 +405,105 @@
     power[...] = jnp.zeros_like(power)
     lined[...] = jnp.zeros_like(lined)
 
-    total = part[me]
-    for j in range(1, n):
-        sent_one[j - 1].wait_recv()
-        total = total + landed[j]
-    line = total[deep * mics : deep * mics + 1]
-    lasts = [
-        jnp.sum(jnp.where(lane == mics * slot + sub, line, 0.0), axis=1, keepdims=True)
-        for slot in range(extra)
-    ]
-    whole = []
-    for slot in range(planes):
-        tile = slot // per_tile
-        plane = turned(total[tile * mics : (tile + 1) * mics], -(slot % per_tile) * width)
-        k, place = slot // mics, slot % mics
-        d = (place + 1) // 2
-        if place == 0 or (place % 2 == 1 and d < half):
-            at_last = lasts[k * (half + 1) + d]
-        elif d == half:
-            at_last = jnp.where(low, lasts[k * (half + 1) + d], 0.0)
-        else:
-            at_last = jnp.zeros((mics, LANES), jnp.float32)
-        whole.append(jnp.where(lane == width, at_last, plane))
-    solved = solve(whole, mics, full, mic_ref[0])
+    upper = mics // 2
+
+    def folded(value):
+        return jnp.where(
+            lane < 2 * width,
+            value,
+            turned(pltpu.roll(value, mics - upper, axis=0), 2 * width),
+        )
+
+    def answer(offset, to, tall):
+        return pltpu.make_async_remote_copy(
+            src_ref=packed.at[:tall],
+            dst_ref=gathered.at[me - base, :tall],
+            send_sem=send_two.at[offset],
+            recv_sem=recv_two.at[me - base],
+            device_id={"tm": to},
+            device_id_type=pl.DeviceIdType.MESH,
+        )
+
+    def answers(act):
+        @pl.when(me == base)
+        def _():
+            for j in range(1, n):
+                act(answer(j, lax.rem(me + j, n), mics))
+
+        @pl.when(solving & (me != base))
+        def _():
+            for j in range(1, n):
+                act(answer(j, lax.rem(me + j, n), upper))
+
+    @pl.when(solving)
+    def _():
+        total = part[me - base]
+        for j in range(1, n):
+            parcel(0, j).wait_recv()
+            total = total + landed[j]
+        line = total[deep * mics : deep * mics + 1]
+        lasts = [
+            jnp.sum(jnp.where(lane == mics * slot + sub, line, 0.0), axis=1, keepdims=True)
+            for slot in range(extra)
+        ]
+        whole = []
+        for slot in range(planes):
+            tile = slot // per_tile
+            plane = turned(total[tile * mics : (tile + 1) * mics], -(slot % per_tile) * width)
+            k, place = slot // mics, slot % mics
+            d = (place + 1) // 2
+            if place == 0 or (place % 2 == 1 and d < half):
+                at_last = lasts[k * (half + 1) + d]
+            elif d == half:
+                at_last = jnp.where(low, lasts[k * (half + 1) + d], 0.0)
+            else:
+                at_last = jnp.zeros((mics, LANES), jnp.float32)
+            whole.append(jnp.where(lane == width, at_last, plane))
+        real, imag = solve(whole, mics, full, mic_ref[0])
+        main = folded(jnp.where(lane < width, real, turned(imag, width)))
+        rest = folded(jnp.where(lane < width, turned(real, -width), imag))
+        sent = jnp.where(sub < upper, main, pltpu.roll(rest, upper, axis=0))
+        packed[...] = sent
+        gathered[me - base] = sent
+
+    answers(lambda copy: copy.start())
+
+    @pl.when(me < n - 1)
+    def _():
+        to_right.wait_send()
+
+    @pl.when(me > 0)
+    def _():
+        to_left.wait_send()
+
+    for to in range(solvers):
+
+        @pl.when(me != base + to)
+        def _():
+            pltpu.make_async_copy(
+                packed.at[: mics if to == 0 else upper],
+                gathered.at[to, : mics if to == 0 else upper],
+                recv_two.at[to],
+            ).wait()
+
+    def unfolded(value):
+        return jnp.where(
+            sub < upper, value, turned(pltpu.roll(value, upper, axis=0), -2 * width)
+        )
+
+    for block in range(tiles):
+        joined = [jnp.zeros((mics, LANES), jnp.float32)] * 2
+        for t in range(per_tile):
+            value = unfolded(gathered[block * per_tile + t])
+            for i in range(2):
+                moved = turned(value, (t - i) * width)
+                joined[i] = moved if t == 0 else jnp.where(lane // width == t, moved, joined[i])
+        for i in range(2):
+            beam[i, :, block * LANES : (block + 1) * LANES] = joined[i]
+    rest = unfolded(pltpu.roll(gathered[0], mics - upper, axis=0))
     for i in range(2):
-        value = jnp.where(lane < width, solved[i], 0.0)
-        for step in (1, 2, 4):
-            value = value + turned(value, step * width)
-        value = jnp.where(lane // width == sub, value, 0.0)
-        packed[i : i + 1, :] = jnp.sum(value, axis=0, keepdims=True)
-    sent_two = []
-    for j in range(1, n):
-        copy = pltpu.make_async_remote_copy(
-            src_ref=packed,
-            dst_ref=gathered.at[me],
-            send_sem=send_two.at[j],
-            recv_sem=recv_two.at[j],
-            device_id={"tm": lax.rem(me + j, n)},
-            device_id_type=pl.DeviceIdType.MESH,
-        )
-        copy.start()
-        sent_two.append(copy)
-    gathered[me] = packed[...]
-    for i in range(2):
-        at_last = jnp.sum(jnp.where(lane == width, solved[i], 0.0), axis=1, keepdims=True)
+        at_last = jnp.sum(jnp.where(lane == i * width, rest, 0.0), axis=1, keepdims=True)
         beam[i, :, MAIN:] = jnp.broadcast_to(at_last, (mics, LANES))
-    to_right.wait_send()
-    to_left.wait_send()
-    for j in range(1, n):
-        sent_two[j - 1].wait_recv()
-    for i in range(2):
-        for block in range(tiles):
-            joined = jnp.zeros((mics, LANES), jnp.float32)
-            for t in range(per_tile):
-                row = gathered[block * per_tile + t, i : i + 1, :]
-                value = jnp.where(lane // width == sub, row, 0.0)
-                for step in (1, 2, 4):
-                    value = value + turned(value, step * width)
-                if mics * width < LANES:
-                    value = turned(value, (t - mics + 1) * width)
-                joined = jnp.where(lane // width == t, value, joined)
-            beam[i, :, block * LANES : (block + 1) * LANES] = joined
 
     load_bank.wait()
     load_repeat.wait()
@@ -428,9 +528,13 @@
         patches,
         first,
     )
-    for j in range(1, n):
-        sent_one[j - 1].wait_send()
-        sent_two[j - 1].wait_send()
+    for to in range(solvers):
+
+        @pl.when(me != base + to)
+        def _():
+            parcel(to, lax.rem(base + to + n - me, n)).wait_send()
+
+    answers(lambda copy: copy.wait_send())
 
 
 def solve(planes, mics, full, ref):
@@ -657,7 +761,8 @@
     smem = pl.BlockSpec(memory_space=pltpu.SMEM)
     anywhere = pl.BlockSpec(memory_space=pltpu.HBM)
     planes = rows * mics
-    deep = -(-planes * (MAIN // n) // LANES)
+    solvers = min(SOLVERS, n)
+    deep = -(-planes * (MAIN // solvers) // LANES)
     tall = deep * mics + 1
     stride = -(-groups // 8) * 8
     q_first = (MELS - 3) // 2 + 1
@@ -681,10 +786,10 @@
             pltpu.VMEM((mics, SPAN), waveform.dtype),
             pltpu.VMEM((mics, reach), waveform.dtype),
             pltpu.VMEM((PADDED // LANES, planes, mics, LANES), jnp.float32),
+            pltpu.VMEM((solvers, tall, LANES), jnp.float32),
             pltpu.VMEM((n, tall, LANES), jnp.float32),
-            pltpu.VMEM((n, tall, LANES), jnp.float32),
-            pltpu.VMEM((2, LANES), jnp.float32),
-            pltpu.VMEM((n, 2, LANES), jnp.float32),
+            pltpu.VMEM((mics, LANES), jnp.float32),
+            pltpu.VMEM((solvers, mics, LANES), jnp.float32),
             pltpu.VMEM((4, mics, mics, LANES), jnp.float32),
             pltpu.VMEM((PADDED, LANES), jnp.float32),
             pltpu.VMEM((LANES, MELS * 8), jnp.bfloat16),

time: 25 us -> 23.2 us (0.928)
  Pallas kernels: 23 us -> 21.1 us
    pallas_call x1, Pallas kernels: 23 us -> 21.1 us  [per_device(): pl.pallas_call(functools.partial(kernel, n), out_shape=jax.ShapeDtypeStru...]
where the time goes in v2:
time: 23.2 us; the launch traced here: 23 us
  Pallas kernels  21.1 us (91%)
  between operations  1.3 us (6%)
  other arithmetic  0.6 us (3%)
    pallas_call x1, Pallas kernels, per_device(): pl.pallas_call(functools.partial(kernel, n), out_shape=jax.ShapeDtypeStru...  21.1 us
    broadcast_in_dim x1, other arithmetic, per_device(): return features.astype(jnp.bfloat16)[None]  0.6 us

profile of v2, /device:TPU:0, one launch (start us, length us, event | category | flops | bytes accessed | tf_op | source)
XLA Modules:
  0.0 23.0 jit_solution(11662767225686271430)
XLA Ops:
  1.3 21.1 %shard_map.127 = f32[16,256]{1,0:T(8,128)S(1)} custom-call(s32[1]{0:T(128)S(6)} %copy.14.valid_ref, s32[1]{0:T(128)S(6)} %copy.15.mic_ref, bf16[8,10240]{1,0:T(8,128)(2,1)} %wave_hbm.1, s32[2,64,257]{2,1,0:T(8,128)} %masks_hbm.1, bf16[512,640]{1,0:T(8,128)(2,1)} %constant.6.clone.table_hbm, f32[384,128]{1,0:T(8,128)} %constant.7.clone.bank_hbm, ...), custom_call_target="tpu_custom_call" | custom-call | tf_op jit(solution)/shard_map/pallas_call | solution.py:770
  22.4 0.6 %convert_bitcast_fusion = bf16[1,16,256]{2,1,0:T(8,128)(2,1)} fusion(f32[16,256]{1,0:T(8,128)S(1)} %shard_map.127), kind=kLoop, calls=%fused_computation | loop fusion | flops 4096 | bytes 24576 | tf_op jit(solution)/shard_map/broadcast_in_dim | solution.py:836

commit v3 on v2

--- a/solution.py
+++ b/solution.py
@@ -21,6 +21,8 @@
 SPAN = GROUP * HOP
 WINDOW = 1024
 SOLVERS = 8
+LEVEL = 32000.0
+TINY = 1e-30
 
 loading = 0.03
 epsilon = 1e-06
@@ -92,7 +94,9 @@
     right,
     cov,
     part,
+    notes,
     landed,
+    noted,
     packed,
     gathered,
     full,
@@ -111,6 +115,8 @@
     nearby_recv,
     send_one,
     recv_one,
+    send_note,
+    recv_note,
     send_two,
     recv_two,
     loads,
@@ -193,7 +199,7 @@
         def _():
             to_right.start()
 
-    late = me >= n // 2
+    late = me >= base + solvers
 
     @pl.when(late)
     def _():
@@ -363,18 +369,32 @@
         line = jnp.where(lane == mics * slot + sub, totals[slot], line)
     line = jnp.sum(line, axis=0, keepdims=True)
     for to in range(solvers):
-        part[to, deep * mics : deep * mics + 1, :] = line
+        notes[to, rows : rows + 1, :] = line
+    group = lane // width
+
+    def packed_for(to, values):
+        packing = values[0]
+        for i in range(1, per_tile):
+            packing = jnp.where(group == (to + i) % per_tile, values[i], packing)
+        return packing
+
     for block in range(tiles):
         totals = adders[block](blocks - 1, tuple(cov[block, slot] for slot in range(planes)))
-        for slot in range(planes):
-            cov[block, slot] = totals[slot]
+        turns = []
+        for k in range(rows):
+            peak = jnp.maximum(jnp.max(totals[k * mics], axis=0, keepdims=True), TINY)
+            peak = jnp.broadcast_to(peak, (mics, LANES))
+            turns.append([turned(peak * (1.0 / LEVEL), i * width) for i in range(per_tile)])
+            scale = LEVEL / peak
+            for slot in range(k * mics, (k + 1) * mics):
+                cov[block, slot] = turned(totals[slot] * scale, slot % per_tile * width)
         for to in range(block * per_tile, (block + 1) * per_tile):
+            for k in range(rows):
+                notes[to, k : k + 1, :] = packed_for(to, turns[k])[:1]
             for tile in range(deep):
-                packing = jnp.zeros((mics, LANES), jnp.float32)
-                for i in range(min(per_tile, planes - tile * per_tile)):
-                    moved = turned(cov[block, tile * per_tile + i], (i - to % per_tile) * width)
-                    packing = moved if i == 0 else jnp.where(lane // width == i, moved, packing)
-                part[to, tile * mics : (tile + 1) * mics, :] = packing
+                values = [cov[block, tile * per_tile + i] for i in range(per_tile)]
+                whole = jnp.round(packed_for(to, values)).astype(jnp.int32)
+                part[to, tile * mics : (tile + 1) * mics, :] = whole.astype(jnp.int16)
 
     def parcel(to, offset):
         return pltpu.make_async_remote_copy(
@@ -386,11 +406,23 @@
             device_id_type=pl.DeviceIdType.MESH,
         )
 
+    def note(to, offset):
+        return pltpu.make_async_remote_copy(
+            src_ref=notes.at[to],
+            dst_ref=noted.at[offset],
+            send_sem=send_note.at[to],
+            recv_sem=recv_note.at[offset],
+            device_id={"tm": base + to},
+            device_id_type=pl.DeviceIdType.MESH,
+        )
+
     for to in range(solvers):
 
         @pl.when(me != base + to)
         def _():
-            parcel(to, lax.rem(base + to + n - me, n)).start()
+            offset = lax.rem(base + to + n - me, n)
+            parcel(to, offset).start()
+            note(to, offset).start()
 
     for load in small:
         load.wait()
@@ -437,11 +469,23 @@
 
     @pl.when(solving)
     def _():
-        total = part[me - base]
+        def levels(codes, held):
+            codes = codes.astype(jnp.int32).astype(jnp.float32)
+            return [
+                codes[tile * mics : (tile + 1) * mics]
+                * held[tile * per_tile // mics : tile * per_tile // mics + 1]
+                for tile in range(deep)
+            ]
+
+        total = levels(part[me - base], notes[me - base])
+        line = notes[me - base, rows : rows + 1]
         for j in range(1, n):
             parcel(0, j).wait_recv()
-            total = total + landed[j]
-        line = total[deep * mics : deep * mics + 1]
+            note(0, j).wait_recv()
+            total = [a + b for a, b in zip(total, levels(landed[j], noted[j]))]
+            line = line + noted[j, rows : rows + 1]
+        back = lax.rem(per_tile - lax.rem(me - base, per_tile), per_tile) * width
+        total = [pltpu.roll(value, back, axis=1) for value in total]
         lasts = [
             jnp.sum(jnp.where(lane == mics * slot + sub, line, 0.0), axis=1, keepdims=True)
             for slot in range(extra)
@@ -449,7 +493,7 @@
         whole = []
         for slot in range(planes):
             tile = slot // per_tile
-            plane = turned(total[tile * mics : (tile + 1) * mics], -(slot % per_tile) * width)
+            plane = turned(total[tile], -(slot % per_tile) * width)
             k, place = slot // mics, slot % mics
             d = (place + 1) // 2
             if place == 0 or (place % 2 == 1 and d < half):
@@ -532,7 +576,8 @@
 
         @pl.when(me != base + to)
         def _():
-            parcel(to, lax.rem(base + to + n - me, n)).wait_send()
+            parcel(to, 0).wait_send()
+            note(to, 0).wait_send()
 
     answers(lambda copy: copy.wait_send())
 
@@ -763,7 +808,7 @@
     planes = rows * mics
     solvers = min(SOLVERS, n)
     deep = -(-planes * (MAIN // solvers) // LANES)
-    tall = deep * mics + 1
+    tall = deep * mics
     stride = -(-groups // 8) * 8
     q_first = (MELS - 3) // 2 + 1
     q_count = q_first * quarter
@@ -786,8 +831,10 @@
             pltpu.VMEM((mics, SPAN), waveform.dtype),
             pltpu.VMEM((mics, reach), waveform.dtype),
             pltpu.VMEM((PADDED // LANES, planes, mics, LANES), jnp.float32),
-            pltpu.VMEM((solvers, tall, LANES), jnp.float32),
-            pltpu.VMEM((n, tall, LANES), jnp.float32),
+            pltpu.VMEM((solvers, tall, LANES), jnp.int16),
+            pltpu.VMEM((solvers, rows + 1, LANES), jnp.float32),
+            pltpu.VMEM((n, tall, LANES), jnp.int16),
+            pltpu.VMEM((n, rows + 1, LANES), jnp.float32),
             pltpu.VMEM((mics, LANES), jnp.float32),
             pltpu.VMEM((solvers, mics, LANES), jnp.float32),
             pltpu.VMEM((4, mics, mics, LANES), jnp.float32),
@@ -804,6 +851,8 @@
             pltpu.VMEM((q_count, 3 * channels), jnp.bfloat16),
             pltpu.SemaphoreType.DMA((2,)),
             pltpu.SemaphoreType.DMA((2,)),
+            pltpu.SemaphoreType.DMA((n,)),
+            pltpu.SemaphoreType.DMA((n,)),
             pltpu.SemaphoreType.DMA((n,)),
             pltpu.SemaphoreType.DMA((n,)),
             pltpu.SemaphoreType.DMA((n,)),

time: 23.2 us -> 22.5 us (0.970)
  Pallas kernels: 21.1 us -> 20.4 us
    pallas_call x1, Pallas kernels: 21.1 us -> 20.4 us  [per_device(): pl.pallas_call(functools.partial(kernel, n), out_shape=jax.ShapeDtypeStru...]
where the time goes in v3:
time: 22.5 us; the launch traced here: 22.3 us
  Pallas kernels  20.4 us (91%)
  between operations  1.3 us (6%)
  other arithmetic  0.6 us (3%)
    pallas_call x1, Pallas kernels, per_device(): pl.pallas_call(functools.partial(kernel, n), out_shape=jax.ShapeDtypeStru...  20.4 us
    broadcast_in_dim x1, other arithmetic, per_device(): return features.astype(jnp.bfloat16)[None]  0.6 us

profile of v3, /device:TPU:0, one launch (start us, length us, event | category | flops | bytes accessed | tf_op | source)
XLA Modules:
  0.0 22.3 jit_solution(14555510879195837493)
XLA Ops:
  1.3 20.4 %shard_map.127 = f32[16,256]{1,0:T(8,128)S(1)} custom-call(s32[1]{0:T(128)S(6)} %copy.14.valid_ref, s32[1]{0:T(128)S(6)} %copy.15.mic_ref, bf16[8,10240]{1,0:T(8,128)(2,1)} %wave_hbm.1, s32[2,64,257]{2,1,0:T(8,128)} %masks_hbm.1, bf16[512,640]{1,0:T(8,128)(2,1)} %constant.6.clone.table_hbm, f32[384,128]{1,0:T(8,128)} %constant.7.clone.bank_hbm, ...), custom_call_target="tpu_custom_call" | custom-call | tf_op jit(solution)/shard_map/pallas_call | solution.py:815
  21.7 0.6 %convert_bitcast_fusion = bf16[1,16,256]{2,1,0:T(8,128)(2,1)} fusion(f32[16,256]{1,0:T(8,128)S(1)} %shard_map.127), kind=kLoop, calls=%fused_computation | loop fusion | flops 4096 | bytes 24576 | tf_op jit(solution)/shard_map/broadcast_in_dim | solution.py:885

commit v4 on v3

--- a/solution.py
+++ b/solution.py
@@ -151,7 +151,7 @@
 
     @pl.when(solving)
     def _():
-        for j in range(1, n):
+        for j in (1, n - 1, *range(2, n - 1)):
             greet(lax.rem(me + j, n))
 
     @pl.when((me > 0) & jnp.logical_not(solving))
@@ -172,7 +172,7 @@
         + counted((me < n - 1) & ((me + 1 < base) | (me + 1 >= base + solvers)))
     )
     to_right = pltpu.make_async_remote_copy(
-        src_ref=wave_hbm.at[:, own - SPAN :],
+        src_ref=wave.at[:, own - SPAN :],
         dst_ref=left,
         send_sem=nearby_send.at[0],
         recv_sem=nearby_recv.at[0],
@@ -180,7 +180,7 @@
         device_id_type=pl.DeviceIdType.MESH,
     )
     to_left = pltpu.make_async_remote_copy(
-        src_ref=wave_hbm.at[:, :reach],
+        src_ref=wave.at[:, :reach],
         dst_ref=right,
         send_sem=nearby_send.at[1],
         recv_sem=nearby_recv.at[1],
@@ -199,7 +199,8 @@
         def _():
             to_right.start()
 
-    late = me >= base + solvers
+    late = (me >= n // 2) & (lax.rem(me, 4) >= 2)
+    load_wave.wait()
 
     @pl.when(late)
     def _():
@@ -218,7 +219,6 @@
         ).astype(jnp.bfloat16)
         return jnp.dot(framed, table[...], preferred_element_type=jnp.float32)
 
-    load_wave.wait()
     ext[:, SPAN : SPAN + own] = wave[...].astype(jnp.float32)
     load_table.wait()
     inner = list(range(1, groups - 1))
@@ -229,7 +229,7 @@
             r * width : (r + 1) * width
         ]
 
-    @pl.when(jnp.logical_not(late))
+    @pl.when(jnp.logical_not(late) & (me >= base))
     def _():
         meet()
 
@@ -329,14 +329,9 @@
         for slot in range(counts[block]):
             cov[block, slot] = totals[slot]
 
-    @pl.when(me > 0)
-    def _():
-        to_right.wait_recv()
-        ext[:, :SPAN] = left[...].astype(jnp.float32)
-
-    @pl.when(me == 0)
-    def _():
-        ext[:, :SPAN] = jnp.zeros((mics, SPAN), jnp.float32)
+    @pl.when(me < base)
+    def _():
+        meet()
 
     @pl.when(me < n - 1)
     def _():
@@ -347,12 +342,14 @@
     def _():
         ext[:, SPAN + own :] = jnp.zeros((mics, reach), jnp.float32)
 
-    found = transform([0, groups - 1])
-    for r in range(GROUP):
-        for i, g in enumerate((0, groups - 1)):
-            at = (r * 2 + i) * mics
-            spec[(r * groups + g) * mics : (r * groups + g + 1) * mics, :] = found[at : at + mics]
-
+    def transform_edge(g):
+        found = transform([g])
+        for r in range(GROUP):
+            spec[(r * groups + g) * mics : (r * groups + g + 1) * mics, :] = found[
+                r * mics : (r + 1) * mics
+            ]
+
+    transform_edge(groups - 1)
     lane = lax.broadcasted_iota(jnp.int32, (mics, LANES), 1)
     sub = lax.broadcasted_iota(jnp.int32, (mics, LANES), 0)
     width = MAIN // solvers
@@ -416,7 +413,8 @@
             device_id_type=pl.DeviceIdType.MESH,
         )
 
-    for to in range(solvers):
+    for turn in range(solvers):
+        to = jnp.where(me < n // 2, solvers - 1 - turn, turn)
 
         @pl.when(me != base + to)
         def _():
@@ -424,6 +422,16 @@
             parcel(to, offset).start()
             note(to, offset).start()
 
+    @pl.when(me > 0)
+    def _():
+        to_right.wait_recv()
+        ext[:, :SPAN] = left[...].astype(jnp.float32)
+
+    @pl.when(me == 0)
+    def _():
+        ext[:, :SPAN] = jnp.zeros((mics, SPAN), jnp.float32)
+
+    transform_edge(0)
     for load in small:
         load.wait()
     channels = conv1_w.shape[1]

time: 22.5 us -> 21.8 us (0.969)
  Pallas kernels: 20.4 us -> 19.7 us
    pallas_call x1, Pallas kernels: 20.4 us -> 19.7 us  [per_device(): pl.pallas_call(functools.partial(kernel, n), out_shape=jax.ShapeDtypeStru...]
where the time goes in v4:
time: 21.8 us; the launch traced here: 21.6 us
  Pallas kernels  19.7 us (90%)
  between operations  1.3 us (6%)
  other arithmetic  0.6 us (3%)
    pallas_call x1, Pallas kernels, per_device(): pl.pallas_call(functools.partial(kernel, n), out_shape=jax.ShapeDtypeStru...  19.7 us
    broadcast_in_dim x1, other arithmetic, per_device(): return features.astype(jnp.bfloat16)[None]  0.6 us

profile of v4, /device:TPU:0, one launch (start us, length us, event | category | flops | bytes accessed | tf_op | source)
XLA Modules:
  0.0 21.6 jit_solution(12828330667957790528)
XLA Ops:
  1.3 19.7 %shard_map.127 = f32[16,256]{1,0:T(8,128)S(1)} custom-call(s32[1]{0:T(128)S(6)} %copy.14.valid_ref, s32[1]{0:T(128)S(6)} %copy.15.mic_ref, bf16[8,10240]{1,0:T(8,128)(2,1)} %wave_hbm.1, s32[2,64,257]{2,1,0:T(8,128)} %masks_hbm.1, bf16[512,640]{1,0:T(8,128)(2,1)} %constant.6.clone.table_hbm, f32[384,128]{1,0:T(8,128)} %constant.7.clone.bank_hbm, ...), custom_call_target="tpu_custom_call" | custom-call | tf_op jit(solution)/shard_map/pallas_call | solution.py:823
  21.0 0.6 %convert_bitcast_fusion = bf16[1,16,256]{2,1,0:T(8,128)(2,1)} fusion(f32[16,256]{1,0:T(8,128)S(1)} %shard_map.127), kind=kLoop, calls=%fused_computation | loop fusion | flops 4096 | bytes 24576 | tf_op jit(solution)/shard_map/broadcast_in_dim | solution.py:893

commit v5 on v4

--- a/solution.py
+++ b/solution.py
@@ -101,6 +101,7 @@
     gathered,
     full,
     bank,
+    split,
     repeat,
     conv2_w,
     proj_w,
@@ -120,6 +121,7 @@
     send_two,
     recv_two,
     loads,
+    taps,
 ):
     rows, frames = masks.shape[0], masks.shape[1]
     mics, own = wave.shape
@@ -135,7 +137,16 @@
     load_wave.start()
     load_table.start()
     load_masks.start()
-    load_conv2 = pltpu.make_async_copy(conv2_hbm, conv2_w, loads.at[3])
+    depth = conv2_hbm.shape[1]
+    load_conv2 = [
+        pltpu.make_async_copy(
+            conv2_hbm.at[3 * late + b],
+            conv2_w.at[b, late * depth : (late + 1) * depth],
+            taps.at[3 * late + b],
+        )
+        for b in range(3)
+        for late in range(3)
+    ]
     load_proj = pltpu.make_async_copy(proj_hbm, proj_w, loads.at[4])
     load_bank = pltpu.make_async_copy(bank_hbm, bank, loads.at[5])
     load_repeat = pltpu.make_async_copy(repeat_hbm, repeat, loads.at[6])
@@ -229,7 +240,7 @@
             r * width : (r + 1) * width
         ]
 
-    @pl.when(jnp.logical_not(late) & (me >= base))
+    @pl.when(jnp.logical_not(late) & (me >= base // 2))
     def _():
         meet()
 
@@ -248,7 +259,8 @@
         load.start()
     load_bank.start()
     load_repeat.start()
-    load_conv2.start()
+    for load in load_conv2:
+        load.start()
     load_proj.start()
 
     load_masks.wait()
@@ -329,7 +341,7 @@
         for slot in range(counts[block]):
             cov[block, slot] = totals[slot]
 
-    @pl.when(me < base)
+    @pl.when(me < base // 2)
     def _():
         meet()
 
@@ -375,7 +387,27 @@
             packing = jnp.where(group == (to + i) % per_tile, values[i], packing)
         return packing
 
-    for block in range(tiles):
+    def parcel(to, offset):
+        return pltpu.make_async_remote_copy(
+            src_ref=part.at[to],
+            dst_ref=landed.at[offset],
+            send_sem=send_one.at[to],
+            recv_sem=recv_one.at[offset],
+            device_id={"tm": base + to},
+            device_id_type=pl.DeviceIdType.MESH,
+        )
+
+    def note(to, offset):
+        return pltpu.make_async_remote_copy(
+            src_ref=notes.at[to],
+            dst_ref=noted.at[offset],
+            send_sem=send_note.at[to],
+            recv_sem=recv_note.at[offset],
+            device_id={"tm": base + to},
+            device_id_type=pl.DeviceIdType.MESH,
+        )
+
+    for block in reversed(range(tiles)):
         totals = adders[block](blocks - 1, tuple(cov[block, slot] for slot in range(planes)))
         turns = []
         for k in range(rows):
@@ -392,35 +424,13 @@
                 values = [cov[block, tile * per_tile + i] for i in range(per_tile)]
                 whole = jnp.round(packed_for(to, values)).astype(jnp.int32)
                 part[to, tile * mics : (tile + 1) * mics, :] = whole.astype(jnp.int16)
-
-    def parcel(to, offset):
-        return pltpu.make_async_remote_copy(
-            src_ref=part.at[to],
-            dst_ref=landed.at[offset],
-            send_sem=send_one.at[to],
-            recv_sem=recv_one.at[offset],
-            device_id={"tm": base + to},
-            device_id_type=pl.DeviceIdType.MESH,
-        )
-
-    def note(to, offset):
-        return pltpu.make_async_remote_copy(
-            src_ref=notes.at[to],
-            dst_ref=noted.at[offset],
-            send_sem=send_note.at[to],
-            recv_sem=recv_note.at[offset],
-            device_id={"tm": base + to},
-            device_id_type=pl.DeviceIdType.MESH,
-        )
-
-    for turn in range(solvers):
-        to = jnp.where(me < n // 2, solvers - 1 - turn, turn)
-
-        @pl.when(me != base + to)
-        def _():
-            offset = lax.rem(base + to + n - me, n)
-            parcel(to, offset).start()
-            note(to, offset).start()
+        for to in reversed(range(block * per_tile, (block + 1) * per_tile)):
+
+            @pl.when(me != base + to)
+            def _():
+                offset = lax.rem(base + to + n - me, n)
+                parcel(to, offset).start()
+                note(to, offset).start()
 
     @pl.when(me > 0)
     def _():
@@ -444,6 +454,12 @@
                 kernel_one[at : at + 1, late * channels : (late + 1) * channels] = tap
     power[...] = jnp.zeros_like(power)
     lined[...] = jnp.zeros_like(lined)
+    load_bank.wait()
+    load_repeat.wait()
+    coarse = bank[:MAIN, :].astype(jnp.bfloat16)
+    split[:MAIN, :] = coarse
+    split[MAIN : 2 * MAIN, :] = (bank[:MAIN, :] - coarse.astype(jnp.float32)).astype(jnp.bfloat16)
+    split[2 * MAIN :, :] = coarse
 
     upper = mics // 2
 
@@ -557,12 +573,11 @@
         at_last = jnp.sum(jnp.where(lane == i * width, rest, 0.0), axis=1, keepdims=True)
         beam[i, :, MAIN:] = jnp.broadcast_to(at_last, (mics, LANES))
 
-    load_bank.wait()
-    load_repeat.wait()
     stem(
         valid_ref[0],
         spec,
         bank,
+        split,
         repeat,
         conv1_b,
         load_conv2,
@@ -681,6 +696,7 @@
     valid,
     spec,
     bank,
+    split,
     repeat,
     conv1_b,
     load_conv2,
@@ -703,7 +719,7 @@
     groups = quarter + 1
     frames = quarter * GROUP
     stride = power.shape[0] // GROUP
-    channels = conv2_w.shape[1]
+    channels = conv2_w.shape[2]
     q_first = (MELS - 3) // 2 + 1
     q_second = (q_first - 3) // 2 + 1
     position = lax.axis_index("tm")
@@ -735,12 +751,14 @@
                 at = r * stride + g
                 power[at : at + 1, lanes] = real * real + imag * imag
 
+    main = power[:, :MAIN]
+    coarse = main.astype(jnp.bfloat16)
+    fine = (main - coarse.astype(jnp.float32)).astype(jnp.bfloat16)
     melspec = (
         jnp.dot(
-            power[:, :MAIN],
-            bank[:MAIN, :],
+            jnp.concatenate([coarse, coarse, fine], axis=1),
+            split[...],
             preferred_element_type=jnp.float32,
-            precision=lax.Precision.HIGHEST,
         )
         + power[:, MAIN:] * bank[MAIN : MAIN + 1, :]
     )
@@ -775,26 +793,23 @@
             one = jnp.where((step == 0) & (position == 0), 0.0, one)
         first[:, lanes] = one.astype(jnp.bfloat16)
 
-    load_conv2.wait()
+    for load in load_conv2:
+        load.wait()
     evens = (q_first + 1) // 2
     summed = jnp.zeros((q_second * quarter, channels), jnp.float32)
     for b in range(3):
         start = {0: 0, 1: evens, 2: 1}[b] * quarter
-        for late in range(3):
-            summed = summed + jnp.dot(
-                first[start : start + q_second * quarter, late * channels : (late + 1) * channels],
-                conv2_w[3 * late + b],
-                preferred_element_type=jnp.float32,
-            )
+        summed = summed + jnp.dot(
+            first[start : start + q_second * quarter, :],
+            conv2_w[b],
+            preferred_element_type=jnp.float32,
+        )
     second = jnp.maximum(summed + conv2_b[...], 0.0).astype(jnp.bfloat16)
     load_proj.wait()
-    out = jnp.zeros((quarter, out_ref.shape[1]), jnp.float32)
-    for r in range(q_second):
-        out = out + jnp.dot(
-            second[r * quarter : (r + 1) * quarter],
-            proj_w[r * channels : (r + 1) * channels, :],
-            preferred_element_type=jnp.float32,
-        )
+    joined = jnp.concatenate(
+        [second[r * quarter : (r + 1) * quarter] for r in range(q_second)], axis=1
+    )
+    out = jnp.dot(joined, proj_w[...], preferred_element_type=jnp.float32)
     out_row = lax.broadcasted_iota(jnp.int32, out.shape, 0) + position * quarter
     out = jnp.where(GROUP * out_row < valid, out + proj_b[...], 0.0)
     out_ref[...] = out
@@ -847,8 +862,9 @@
             pltpu.VMEM((solvers, mics, LANES), jnp.float32),
             pltpu.VMEM((4, mics, mics, LANES), jnp.float32),
             pltpu.VMEM((PADDED, LANES), jnp.float32),
+            pltpu.VMEM((3 * MAIN, LANES), jnp.bfloat16),
             pltpu.VMEM((LANES, MELS * 8), jnp.bfloat16),
-            pltpu.VMEM(conv2_w.shape, jnp.bfloat16),
+            pltpu.VMEM((3, 3 * channels, channels), jnp.bfloat16),
             pltpu.VMEM(proj_w.shape, jnp.bfloat16),
             pltpu.VMEM((2, mics, PADDED), jnp.float32),
             pltpu.VMEM((GROUP * stride, PADDED), jnp.float32),
@@ -866,6 +882,7 @@
             pltpu.SemaphoreType.DMA((n,)),
             pltpu.SemaphoreType.DMA((n,)),
             pltpu.SemaphoreType.DMA((11,)),
+            pltpu.SemaphoreType.DMA((9,)),
         ],
         compiler_params=pltpu.CompilerParams(
             collective_id=0, has_side_effects=True, vmem_limit_bytes=16 << 20

time: 21.8 us -> 21.5 us (0.986)
    pallas_call x1, Pallas kernels: 19.7 us -> 19.5 us  [per_device(): pl.pallas_call(functools.partial(kernel, n), out_shape=jax.ShapeDtypeStru...]
where the time goes in v5:
time: 21.5 us; the launch traced here: 21.4 us
  Pallas kernels  19.5 us (91%)
  between operations  1.3 us (6%)
  other arithmetic  0.6 us (3%)
    pallas_call x1, Pallas kernels, per_device(): pl.pallas_call(functools.partial(kernel, n), out_shape=jax.ShapeDtypeStru...  19.5 us
    broadcast_in_dim x1, other arithmetic, per_device(): return features.astype(jnp.bfloat16)[None]  0.6 us

profile of v5, /device:TPU:0, one launch (start us, length us, event | category | flops | bytes accessed | tf_op | source)
XLA Modules:
  0.0 21.4 jit_solution(2711049909345432444)
XLA Ops:
  1.3 19.5 %shard_map.127 = f32[16,256]{1,0:T(8,128)S(1)} custom-call(s32[1]{0:T(128)S(6)} %copy.14.valid_ref, s32[1]{0:T(128)S(6)} %copy.15.mic_ref, bf16[8,10240]{1,0:T(8,128)(2,1)} %wave_hbm.1, s32[2,64,257]{2,1,0:T(8,128)} %masks_hbm.1, bf16[512,640]{1,0:T(8,128)(2,1)} %constant.6.clone.table_hbm, f32[384,128]{1,0:T(8,128)} %constant.7.clone.bank_hbm, ...), custom_call_target="tpu_custom_call" | custom-call | tf_op jit(solution)/shard_map/pallas_call | solution.py:838
  20.8 0.6 %convert_bitcast_fusion = bf16[1,16,256]{2,1,0:T(8,128)(2,1)} fusion(f32[16,256]{1,0:T(8,128)S(1)} %shard_map.127), kind=kLoop, calls=%fused_computation | loop fusion | flops 4096 | bytes 24576 | tf_op jit(solution)/shard_map/broadcast_in_dim | solution.py:910

commit v6 on v5

--- a/solution.py
+++ b/solution.py
@@ -210,7 +210,7 @@
         def _():
             to_right.start()
 
-    late = (me >= n // 2) & (lax.rem(me, 4) >= 2)
+    late = me >= n - 2
     load_wave.wait()
 
     @pl.when(late)
@@ -315,30 +315,34 @@
                     place += 1
         return tuple(totals)
 
-    def add_last_bin(h, totals):
-        totals = list(totals)
-        span, places = frames_of(h)
-        held = [weight[k, span, pl.ds(MAIN, LANES)] for k in range(rows)]
-        for i, at in enumerate(places):
-            re = spec[at, pl.ds(2 * MAIN, LANES)]
-            for d in range(half + 1):
-                product = re * (re if d == 0 else pltpu.roll(re, mics - d, axis=0))
-                for k in range(rows):
-                    slot = k * (half + 1) + d
-                    totals[slot] = totals[slot] + held[k][i : i + 1] * product
-        return tuple(totals)
+    across = lax.broadcasted_iota(jnp.int32, (mics, LANES), 1)
+
+    def spread_last_bin(chosen, held):
+        parts = [held] + [jnp.zeros((mics, LANES), jnp.float32)] * (GROUP - 1)
+        for g in chosen:
+            for r in range(GROUP):
+                value = spec[pl.ds((r * groups + g) * mics, mics), pl.ds(2 * MAIN, LANES)]
+                parts[r] = jnp.where(across == (g - 1) * GROUP + r, value, parts[r])
+        return (parts[0] + parts[1]) + (parts[2] + parts[3])
+
+    diagonal = lax.broadcasted_iota(jnp.int32, (frames, LANES), 0) == lax.broadcasted_iota(
+        jnp.int32, (frames, LANES), 1
+    )
+    last_weight = [
+        jnp.sum(jnp.where(diagonal, weight[k, :, MAIN:], 0.0), axis=0, keepdims=True)
+        for k in range(rows)
+    ]
+    last_bin = spread_last_bin(inner, jnp.zeros((mics, LANES), jnp.float32))
 
     blocks = frames // (2 * GROUP)
     tiles = MAIN // LANES
     planes = rows * mics
     extra = rows * (half + 1)
     adders = [functools.partial(add_block, block=block) for block in range(tiles)]
-    adders.append(add_last_bin)
-    counts = [planes] * tiles + [extra]
-    for block in range(tiles + 1):
-        zeros = tuple(jnp.zeros((mics, LANES), jnp.float32) for _ in range(counts[block]))
+    for block in range(tiles):
+        zeros = tuple(jnp.zeros((mics, LANES), jnp.float32) for _ in range(planes))
         totals = lax.fori_loop(0, blocks - 1, adders[block], zeros)
-        for slot in range(counts[block]):
+        for slot in range(planes):
             cov[block, slot] = totals[slot]
 
     @pl.when(me < base // 2)
@@ -372,7 +376,12 @@
         amount = amount % LANES
         return pltpu.roll(value, amount, axis=1) if amount else value
 
-    totals = add_last_bin(blocks - 1, tuple(cov[tiles, slot] for slot in range(extra)))
+    last_bin = spread_last_bin([groups - 1], last_bin)
+    totals = []
+    for k in range(rows):
+        for d in range(half + 1):
+            product = last_bin * (last_bin if d == 0 else pltpu.roll(last_bin, mics - d, axis=0))
+            totals.append(jnp.sum(product * last_weight[k], axis=1, keepdims=True))
     line = jnp.zeros((mics, LANES), jnp.float32)
     for slot in range(extra):
         line = jnp.where(lane == mics * slot + sub, totals[slot], line)
@@ -470,26 +479,28 @@
             turned(pltpu.roll(value, mics - upper, axis=0), 2 * width),
         )
 
-    def answer(offset, to, tall):
+    def answer(to, tall):
         return pltpu.make_async_remote_copy(
             src_ref=packed.at[:tall],
             dst_ref=gathered.at[me - base, :tall],
-            send_sem=send_two.at[offset],
+            send_sem=send_two.at[to],
             recv_sem=recv_two.at[me - base],
             device_id={"tm": to},
             device_id_type=pl.DeviceIdType.MESH,
         )
 
     def answers(act):
-        @pl.when(me == base)
-        def _():
-            for j in range(1, n):
-                act(answer(j, lax.rem(me + j, n), mics))
-
-        @pl.when(solving & (me != base))
-        def _():
-            for j in range(1, n):
-                act(answer(j, lax.rem(me + j, n), upper))
+        for to in range(n):
+
+            if to != base:
+
+                @pl.when(me == base)
+                def _():
+                    act(answer(to, mics))
+
+            @pl.when(solving & (me != base) & (me != to))
+            def _():
+                act(answer(to, upper))
 
     @pl.when(solving)
     def _():
@@ -853,7 +864,7 @@
             pltpu.VMEM((GROUP * groups * mics, SPECTRUM), jnp.float32),
             pltpu.VMEM((mics, SPAN), waveform.dtype),
             pltpu.VMEM((mics, reach), waveform.dtype),
-            pltpu.VMEM((PADDED // LANES, planes, mics, LANES), jnp.float32),
+            pltpu.VMEM((MAIN // LANES, planes, mics, LANES), jnp.float32),
             pltpu.VMEM((solvers, tall, LANES), jnp.int16),
             pltpu.VMEM((solvers, rows + 1, LANES), jnp.float32),
             pltpu.VMEM((n, tall, LANES), jnp.int16),

time: 21.5 us -> 21.5 us (level)
  no operation moved by 1% of the time
where the time goes in v6:
time: 21.5 us; the launch traced here: 21.3 us
  Pallas kernels  19.4 us (90%)
  between operations  1.3 us (6%)
  other arithmetic  0.6 us (3%)
    pallas_call x1, Pallas kernels, per_device(): pl.pallas_call(functools.partial(kernel, n), out_shape=jax.ShapeDtypeStru...  19.4 us
    broadcast_in_dim x1, other arithmetic, per_device(): return features.astype(jnp.bfloat16)[None]  0.6 us

profile of v6, /device:TPU:0, one launch (start us, length us, event | category | flops | bytes accessed | tf_op | source)
XLA Modules:
  0.0 21.3 jit_solution(5668864289957942560)
XLA Ops:
  1.3 19.4 %shard_map.127 = f32[16,256]{1,0:T(8,128)S(1)} custom-call(s32[1]{0:T(128)S(6)} %copy.14.valid_ref, s32[1]{0:T(128)S(6)} %copy.15.mic_ref, bf16[8,10240]{1,0:T(8,128)(2,1)} %wave_hbm.1, s32[2,64,257]{2,1,0:T(8,128)} %masks_hbm.1, bf16[512,640]{1,0:T(8,128)(2,1)} %constant.6.clone.table_hbm, f32[384,128]{1,0:T(8,128)} %constant.7.clone.bank_hbm, ...), custom_call_target="tpu_custom_call" | custom-call | tf_op jit(solution)/shard_map/pallas_call | solution.py:849
  20.7 0.6 %convert_bitcast_fusion = bf16[1,16,256]{2,1,0:T(8,128)(2,1)} fusion(f32[16,256]{1,0:T(8,128)S(1)} %shard_map.127), kind=kLoop, calls=%fused_computation | loop fusion | flops 4096 | bytes 24576 | tf_op jit(solution)/shard_map/broadcast_in_dim | solution.py:921

commit v7 on v6

--- a/solution.py
+++ b/solution.py
@@ -210,7 +210,7 @@
         def _():
             to_right.start()
 
-    late = me >= n - 2
+    late = (me >= n // 2) & (lax.rem(me, 4) >= 2)
     load_wave.wait()
 
     @pl.when(late)

time: 21.5 us -> 21.5 us (level)
  no operation moved by 1% of the time
where the time goes in v7:
time: 21.5 us; the launch traced here: 21.3 us
  Pallas kernels  19.4 us (90%)
  between operations  1.3 us (6%)
  other arithmetic  0.6 us (3%)
    pallas_call x1, Pallas kernels, per_device(): pl.pallas_call(functools.partial(kernel, n), out_shape=jax.ShapeDtypeStru...  19.4 us
    broadcast_in_dim x1, other arithmetic, per_device(): return features.astype(jnp.bfloat16)[None]  0.6 us

profile of v7, /device:TPU:0, one launch (start us, length us, event | category | flops | bytes accessed | tf_op | source)
XLA Modules:
  0.0 21.3 jit_solution(6569437377648634479)
XLA Ops:
  1.3 19.4 %shard_map.127 = f32[16,256]{1,0:T(8,128)S(1)} custom-call(s32[1]{0:T(128)S(6)} %copy.14.valid_ref, s32[1]{0:T(128)S(6)} %copy.15.mic_ref, bf16[8,10240]{1,0:T(8,128)(2,1)} %wave_hbm.1, s32[2,64,257]{2,1,0:T(8,128)} %masks_hbm.1, bf16[512,640]{1,0:T(8,128)(2,1)} %constant.6.clone.table_hbm, f32[384,128]{1,0:T(8,128)} %constant.7.clone.bank_hbm, ...), custom_call_target="tpu_custom_call" | custom-call | tf_op jit(solution)/shard_map/pallas_call | solution.py:849
  20.7 0.6 %convert_bitcast_fusion = bf16[1,16,256]{2,1,0:T(8,128)(2,1)} fusion(f32[16,256]{1,0:T(8,128)S(1)} %shard_map.127), kind=kLoop, calls=%fused_computation | loop fusion | flops 4096 | bytes 24576 | tf_op jit(solution)/shard_map/broadcast_in_dim | solution.py:921
